TPU v7x, 128 devices: a whole 4x4x4 slice. The times are simulated.
128 devices in a mesh: map: 16 (over y, x), rep: 8 (over z, core).
Axes of the slice: x: 4, y: 4, z: 4, core: 2. Of those that a mesh axis runs over, the one named last changes fastest.
Arguments:
- amplitudes: float32 [2, 4096, 5120], P(None, ('map', 'rep')), may hold values from -6 to 6
- integrals: float32 [2, 5120, 5120], P(None, None, ('map', 'rep')), may hold values from -0.078125 to 0.078125
- row_gap: float32 [2, 4096], P(None, ('map', 'rep')), may hold values from 0.5 to 4
- col_gap: float32 [2, 5120], replicated, may hold values from 0.5 to 4
Outputs:
- update: float32 [2, 4096, 5120], P(None, ('map', 'rep'))
All inputs are finite; a program needn't handle non-finite values.
Results may differ from a plain program's by a relative error of at most 0.00007.
Values sent between devices are 32-bit elements; how exact they have to be, the bound alone decides.
No kernel may reach another device: no remote copies, remote signals or barrier semaphores. Data moves between devices by JAX's collectives and lax.ppermute only.
A program may use at most 128 MiB of HBM per device.

v0:
```python
import jax
import jax.numpy as jnp
from jax import lax
from jax.sharding import PartitionSpec as P


def per_device(amplitudes, integrals, row_gap, col_gap):
    amp_block = lax.all_to_all(amplitudes, "rep", split_axis=2, concat_axis=1, tiled=True)
    int_block = lax.all_to_all(integrals, "rep", split_axis=1, concat_axis=2, tiled=True)
    partial_value = jnp.einsum(
        "gsk,gkc->gsc",
        amp_block,
        lax.all_gather(int_block, "map", axis=2, tiled=True),
        precision=lax.Precision.HIGHEST,
        preferred_element_type=jnp.float32,
    )
    product = lax.psum_scatter(partial_value, "rep", scatter_dimension=1, tiled=True)
    return product / (row_gap[:, :, None] + col_gap[:, None, :])


def solution(mesh):
    placed = (
        P(None, ("map", "rep"), None),
        P(None, None, ("map", "rep")),
        P(None, ("map", "rep")),
        P(),
    )
    return jax.shard_map(
        per_device,
        mesh=mesh,
        in_specs=placed,
        out_specs=P(None, ("map", "rep"), None),
        check_vma=False,
    )
```

profile of v0, /device:TPU:1, one launch (start us, length us, event | category | flops | bytes accessed | tf_op | source)
XLA Modules:
  0.0 337.0 jit_solution(603539111832813769)
XLA Ops:
  6.5 0.0 all-gather.2.cloned.1.call-start
  6.5 6.9 %copy.9 = f32[2,5120,40]{2,0,1:T(2,128)} copy(f32[2,5120,40]{1,2,0:T(8,128)} %param.5) | data formatting | bytes 3276800 | tf_op args[1]
  13.5 10.8 %reshape.4 = f32[8,1,51200]{2,1,0:T(1,128)S(1)} reshape(f32[5120,2,40]{2,1,0:T(2,128)} %bitcast.17) | data formatting | bytes 3276800
  24.3 28.4 %all_to_all.36 = f32[8,1,51200]{2,1,0:T(1,128)S(1)} all-to-all(f32[8,1,51200]{2,1,0:T(1,128)S(1)} %reshape.4), channel_id=1, replica_groups=mesh['map'=16,'rep'=8] {'rep'}, dimensions={0} | all-to-all | bytes 3276800 | tf_op jit(solution)/shard_map/all_to_all | solution.py:9
  52.7 0.5 broadcast.2
  53.2 4.5 %reduce.1 = f32[8,51200]{1,0:T(8,128)S(1)} reduce(f32[8,1,51200]{2,1,0:T(1,128)S(1)} %all_to_all.36, f32[]{:T(128)} %broadcast.2), dimensions={1}, to_apply=%all_to_all.30.reduce_sub_computation | reduce | bytes 3276804 | tf_op jit(solution)/shard_map/all_to_all | solution.py:9
  57.7 11.4 %reshape.5 = f32[5120,2,40]{2,1,0:T(2,128)} reshape(f32[8,51200]{1,0:T(8,128)S(1)} %reduce.1) | data formatting | bytes 3276800
  69.2 6.9 %copy.10 = f32[2,8,640,40]{2,3,1,0:T(8,128)} copy(f32[2,8,640,40]{3,0,2,1:T(2,128)} %bitcast.16) | data formatting | bytes 3276800 | tf_op jit(solution)/shard_map/all_to_all | solution.py:9
  76.0 0.0 copy-start
  76.0 0.0 all-gather.2.cloned.1.call-update
  76.1 0.2 reduce-scatter.2.cloned.1.call-start
  76.3 1.1 copy-done
  77.4 4.7 %copy.7 = f32[2,32,5120]{1,0,2:T(2,128)} copy(f32[2,32,5120]{2,1,0:T(8,128)S(1)} %copy-done) | data formatting | bytes 2621440 | tf_op args[0]
  82.0 6.8 %reshape.2 = f32[8,1,40960]{2,1,0:T(1,128)S(1)} reshape(f32[5120,2,32]{2,1,0:T(2,128)} %bitcast.15) | data formatting | bytes 2621440
  88.9 21.1 %all_to_all.37 = f32[8,1,40960]{2,1,0:T(1,128)S(1)} all-to-all(f32[8,1,40960]{2,1,0:T(1,128)S(1)} %reshape.2), channel_id=1, replica_groups=mesh['map'=16,'rep'=8] {'rep'}, dimensions={0} | all-to-all | bytes 2621440 | tf_op jit(solution)/shard_map/all_to_all | solution.py:8
  110.0 3.8 %reduce = f32[8,40960]{1,0:T(8,128)S(1)} reduce(f32[8,1,40960]{2,1,0:T(1,128)S(1)} %all_to_all.37, f32[]{:T(128)} %broadcast.2), dimensions={1}, to_apply=%all_to_all.26.reduce_sub_computation | reduce | bytes 2621444 | tf_op jit(solution)/shard_map/all_to_all | solution.py:8
  113.8 6.8 %reshape.3 = f32[5120,2,32]{2,1,0:T(2,128)} reshape(f32[8,40960]{1,0:T(8,128)S(1)} %reduce) | data formatting | bytes 2621440
  120.6 5.5 %copy.8 = f32[2,32,8,640]{3,1,2,0:T(8,128)S(1)} copy(f32[2,32,8,640]{1,0,3,2:T(2,128)} %bitcast.14) | data formatting | bytes 2621440 | tf_op jit(solution)/shard_map/all_to_all | solution.py:8
  126.1 109.1 %all-gather.2.cloned.1.call-done = f32[2,640,5120]{1,2,0:T(8,128)} async-done(((f32[2,640,320]{1,2,0:T(8,128)}), f32[2,640,5120]{1,2,0:T(8,128)}) %all-gather.2.cloned.1.call-update) | async-done | bytes 26214416 | tf_op jit(solution)/shard_map/all_gather | solution.py:13
  235.2 30.5 %fusion = f32[2,256,5120]{2,1,0:T(8,128)} fusion(f32[2,256,640]{2,1,0:T(8,128)S(1)} %bitcast.19, f32[2,640,5120]{1,2,0:T(8,128)} %all-gather.2.cloned.1.call-done), kind=kOutput, calls=%fused_computation.1 | convolution fusion | flops 20132659200 | bytes 38010880 | tf_op jit(solution)/shard_map/gsk,gkc->gsc/dot_general | solution.py:10
  265.7 0.0 copy-start.1
  265.7 0.0 copy-start.2
  265.7 0.0 reduce-scatter.2.cloned.1.call-update
  265.7 61.8 %reduce-scatter.2.cloned.1.call-done = f32[2,32,5120]{2,1,0:T(8,128)} async-done(((f32[2,256,5120]{2,1,0:T(8,128)}), f32[2,32,5120]{2,1,0:T(8,128)}) %reduce-scatter.2.cloned.1.call-update) | async-done | bytes 1310736 | tf_op jit(solution)/shard_map/reduce_scatter | solution.py:17
  327.5 0.0 copy-done.1
  327.5 0.0 copy-done.2
  327.5 2.6 add_divide_fusion
Async XLA Ops:
  6.5 228.7 %all-gather.2.cloned.1.call-start = ((), (), s32[]{:S(2)}) async-start(), calls=%async_computation.3 | async-start | bytes 27852800 | tf_op jit(solution)/shard_map/all_gather | solution.py:13
  76.0 1.3 copy-start
  76.1 251.4 %reduce-scatter.2.cloned.1.call-start = ((), (), s32[]{:S(2)}) async-start(), calls=%async_computation.4 | async-start | bytes 11796480 | tf_op jit(solution)/shard_map/reduce_scatter | solution.py:17
  265.7 61.8 %copy-start.1 = (f32[2,5120]{1,0:T(2,128)S(1)}, f32[2,5120]{1,0:T(2,128)}, u32[]{:S(2)}) copy-start(f32[2,5120]{1,0:T(2,128)} %param.7) | copy-start | bytes 122884
  265.7 61.8 %copy-start.2 = (f32[2,32]{1,0:T(2,128)S(1)}, f32[2,32]{1,0:T(2,128)}, u32[]{:S(2)}) copy-start(f32[2,32]{1,0:T(2,128)} %param.6) | copy-start | bytes 772
Sparse Core Ops, SparseCore 0:
  76.2 158.9 all-gather.1
  265.8 61.6 reduce-scatter.1
where the time goes:
time: 338 us; the launch traced here: 337 us
  waiting for transfers between devices  171 us (51%)
  local copies, waits for them, and re-layouts  61.5 us (18%)
  blocking collectives  49.5 us (15%)
  matrix products  30.5 us (9%)
  between operations  13.4 us (4%)
  other arithmetic  10.9 us (3%)
    all_gather x1, waiting for transfers between devices, per_device(): lax.all_gather(int_block, 'map', axis=2, tiled=True)  109 us
    reduce_scatter x1, waiting for transfers between devices, per_device(): lax.psum_scatter(partial_value, 'rep', scatter_dimension=1, tiled=True)  61.8 us
    unnamed x12, local copies, waits for them, and re-layouts  48.6 us
    dot_general x1, matrix products, per_device(): jnp.einsum('gsk,gkc->gsc', amp_block, lax.all_gather(int_block, 'map', ax...  30.5 us
    all_to_all x1, blocking collectives, per_device(): lax.all_to_all(integrals, 'rep', split_axis=1, concat_axis=2, tiled=True)  28.4 us
    all_to_all x1, blocking collectives, per_device(): lax.all_to_all(amplitudes, 'rep', split_axis=2, concat_axis=1, tiled=True)  21.1 us
    all_to_all x1, local copies, waits for them, and re-layouts, per_device(): lax.all_to_all(integrals, 'rep', split_axis=1, concat_axis=2, tiled=True)  6.88 us
  transfers between devices with their start and end apart: 2, of which 2 were waited for; matrix products, arithmetic and copies ran while one was open for 8% of the time, Pallas kernels for 0%

commit v1 on v0

--- a/solution.py
+++ b/solution.py
@@ -2,6 +2,10 @@
 import jax.numpy as jnp
 from jax import lax
 from jax.sharding import PartitionSpec as P
+
+assign_surface = lambda a0: jnp.concatenate(
+    jax.lax.all_to_all(jnp.stack([a0 for _ in range(jax.lax.psum(1, "map"))], 0), "map", 0, 0), 2
+)
 
 
 def per_device(amplitudes, integrals, row_gap, col_gap):
@@ -10,7 +14,7 @@
     partial_value = jnp.einsum(
         "gsk,gkc->gsc",
         amp_block,
-        lax.all_gather(int_block, "map", axis=2, tiled=True),
+        assign_surface(int_block),
         precision=lax.Precision.HIGHEST,
         preferred_element_type=jnp.float32,
     )

time: 338 us -> 603 us (1.78)
  waiting for transfers between devices: 171 us -> 444 us
  blocking collectives: 49.5 us -> 0 us
  local copies, waits for them, and re-layouts: 61.5 us -> 81.3 us
  starting transfers between devices: 0.22 us -> 19.5 us
    all_to_all x0 -> x3, waiting for transfers between devices: none -> 385 us  [the longest x1 376 us: jax.lax.all_to_all(jnp.stack([a0 for _ in range(jax.lax.psum(1, 'map'))],...]
    all_gather x1 -> x0, waiting for transfers between devices: 109 us -> none  [per_device(): lax.all_gather(int_block, 'map', axis=2, tiled=True)]
    all_to_all x2 -> x0, blocking collectives: 49.5 us -> none  [the longest x1 28.4 us: per_device(): lax.all_to_all(integrals, 'rep', split_axis=1, concat_axis=2, tiled=True)]
    all_to_all x0 -> x3, starting transfers between devices: none -> 19.3 us  [the longest x1 6.95 us: per_device(): lax.all_to_all(integrals, 'rep', split_axis=1, concat_axis=2, tiled=True)]
    another operation x0 -> x1, local copies, waits for them, and re-layouts: none -> 11.6 us  [jnp.stack([a0 for _ in range(jax.lax.psum(1, 'map'))], 0)]
    all_to_all x0 -> x1, local copies, waits for them, and re-layouts: none -> 9.42 us  [jax.lax.all_to_all(jnp.stack([a0 for _ in range(jax.lax.psum(1, 'map'))],...]
  transfers between devices with their start and end apart: 2 -> 4, of which waited for: 2 -> 3; matrix products, arithmetic and copies ran while one was open for 8% -> 9% of each run, Pallas kernels for 0% -> 0%
where the time goes in v1:
time: 603 us; the launch traced here: 599 us
  waiting for transfers between devices  444 us (74%)
  local copies, waits for them, and re-layouts  81.3 us (13%)
  matrix products  28.6 us (5%)
  starting transfers between devices  19.5 us (3%)
  between operations  13.7 us (2%)
  other arithmetic  12.3 us (2%)
    all_to_all x1, waiting for transfers between devices, jax.lax.all_to_all(jnp.stack([a0 for _ in range(jax.lax.psum(1, 'map'))],...  376 us
    reduce_scatter x1, waiting for transfers between devices, per_device(): lax.psum_scatter(partial_value, 'rep', scatter_dimension=1, tiled=True)  58.5 us
    unnamed x12, local copies, waits for them, and re-layouts  48.6 us
    dot_general x1, matrix products, per_device(): jnp.einsum('gsk,gkc->gsc', amp_block, assign_surface(int_block), precisio...  28.6 us
  transfers between devices with their start and end apart: 4, of which 3 were waited for; matrix products, arithmetic and copies ran while one was open for 9% of the time, Pallas kernels for 0%

profile of v1, /device:TPU:1, one launch (start us, length us, event | category | flops | bytes accessed | tf_op | source)
XLA Modules:
  0.0 599.4 jit_solution(11074479332016169882)
XLA Ops:
  6.5 6.9 %copy.13 = f32[2,5120,40]{2,0,1:T(2,128)} copy(f32[2,5120,40]{1,2,0:T(8,128)} %param.5) | data formatting | bytes 3276800 | tf_op args[1]
  13.4 11.5 %reshape.15 = f32[8,1,51200]{2,1,0:T(1,128)} reshape(f32[5120,2,40]{2,1,0:T(2,128)} %bitcast.22) | data formatting | bytes 3276800
  25.0 0.0 copy-start
  25.0 6.9 %all-to-all-start.1 = ((f32[8,1,51200]{2,1,0:T(1,128)}), f32[8,1,51200]{2,1,0:T(1,128)S(1)}, u32[]{:S(2)}, u32[]{:S(2)}) async-start(f32[8,1,51200]{2,1,0:T(1,128)} %reshape.15), calls=%async_computation.1 | async-start | bytes 3276800 | tf_op jit(solution)/shard_map/all_to_all | solution.py:13
  31.9 0.0 copy-done
  31.9 4.7 copy.11
  36.6 7.4 %reshape.13 = f32[8,1,40960]{2,1,0:T(1,128)} reshape(f32[5120,2,32]{2,1,0:T(2,128)} %bitcast.20) | data formatting | bytes 2621440
  44.0 9.3 %all-to-all-done.1 = f32[8,1,51200]{2,1,0:T(1,128)S(1)} async-done(((f32[8,1,51200]{2,1,0:T(1,128)}), f32[8,1,51200]{2,1,0:T(1,128)S(1)}, u32[]{:S(2)}, u32[]{:S(2)}) %all-to-all-start.1) | async-done | bytes 1638432 | tf_op jit(solution)/shard_map/all_to_all | solution.py:13
  53.3 5.5 all-to-all-start
  58.9 0.6 broadcast.3
  59.5 4.6 reduce.1
  64.1 11.4 %reshape.16 = f32[5120,2,40]{2,1,0:T(2,128)} reshape(f32[8,51200]{1,0:T(8,128)S(1)} %reduce.1) | data formatting | bytes 3276800
  75.5 5.5 copy.20
  81.0 0.0 all-to-all-done
  81.0 11.6 %stack.5 = f32[16,2,640,320]{2,3,1,0:T(8,128)} broadcast(f32[2,640,320]{1,2,0:T(8,128)S(1)} %bitcast.23), dimensions={1,2,3} | broadcast | bytes 27852800 | tf_op jit(solution)/shard_map/stack | solution.py:7
  92.6 6.8 %all-to-all-start.2 = ((f32[16,2,640,320]{2,3,1,0:T(8,128)}), f32[16,2,640,320]{2,3,1,0:T(8,128)}, u32[]{:S(2)}, u32[]{:S(2)}) async-start(f32[16,2,640,320]{2,3,1,0:T(8,128)} %stack.5), calls=%async_computation.2 | async-start | bytes 52428800 | tf_op jit(solution)/shard_map/all_to_all | solution.py:7
  99.4 0.2 reduce-scatter.2.cloned.1.call-start
  99.6 5.1 reduce
  104.8 6.7 %reshape.14 = f32[5120,2,32]{2,1,0:T(2,128)} reshape(f32[8,40960]{1,0:T(8,128)S(1)} %reduce) | data formatting | bytes 2621440
  111.5 5.5 copy.12
  117.0 376.2 %all-to-all-done.2 = f32[16,2,640,320]{2,3,1,0:T(8,128)} async-done(((f32[16,2,640,320]{2,3,1,0:T(8,128)}), f32[16,2,640,320]{2,3,1,0:T(8,128)}, u32[]{:S(2)}, u32[]{:S(2)}) %all-to-all-start.2) | async-done | bytes 26214432 | tf_op jit(solution)/shard_map/all_to_all | solution.py:7
  493.2 9.4 %copy.16 = f32[16,2,640,320]{2,3,0,1:T(8,128)S(1)} copy(f32[16,2,640,320]{2,3,1,0:T(8,128)} %all-to-all-done.2) | data formatting | bytes 52428800 | tf_op jit(solution)/shard_map/all_to_all | solution.py:7
  502.6 28.6 %fusion = f32[2,256,5120]{2,1,0:T(8,128)} fusion(f32[2,256,640]{2,1,0:T(8,128)S(1)} %bitcast.24, f32[2,640,5120]{1,2,0:T(8,128)S(1)} %bitcast.18), kind=kOutput, calls=%fused_computation.1 | convolution fusion | flops 20132659200 | bytes 38010880 | tf_op jit(solution)/shard_map/gsk,gkc->gsc/dot_general | solution.py:14
  531.2 0.0 copy-start.1
  531.2 0.0 copy-start.2
  531.2 0.0 reduce-scatter.2.cloned.1.call-update
  531.2 58.5 %reduce-scatter.2.cloned.1.call-done = f32[2,32,5120]{2,1,0:T(8,128)} async-done(((f32[2,256,5120]{2,1,0:T(8,128)}), f32[2,32,5120]{2,1,0:T(8,128)}) %reduce-scatter.2.cloned.1.call-update) | async-done | bytes 1310736 | tf_op jit(solution)/shard_map/reduce_scatter | solution.py:21
  589.7 0.0 copy-done.1
  589.7 0.0 copy-done.2
  589.7 2.6 add_divide_fusion
Async XLA Ops:
  25.0 7.0 %copy-start = (f32[2,32,5120]{2,1,0:T(8,128)S(1)}, f32[2,32,5120]{2,1,0:T(8,128)}, u32[]{:S(2)}) copy-start(f32[2,32,5120]{2,1,0:T(8,128)} %param.4) | copy-start | bytes 3932164
  25.0 28.4 %all-to-all-start.1 = ((f32[8,1,51200]{2,1,0:T(1,128)}), f32[8,1,51200]{2,1,0:T(1,128)S(1)}, u32[]{:S(2)}, u32[]{:S(2)}) async-start(f32[8,1,51200]{2,1,0:T(1,128)} %reshape.15), calls=%async_computation.1 | async-start | bytes 3276800 | tf_op jit(solution)/shard_map/all_to_all | solution.py:13
  53.3 27.7 %all-to-all-start = ((f32[8,1,40960]{2,1,0:T(1,128)}), f32[8,1,40960]{2,1,0:T(1,128)}, u32[]{:S(2)}, u32[]{:S(2)}) async-start(f32[8,1,40960]{2,1,0:T(1,128)} %reshape.13), calls=%async_computation | async-start | bytes 2621440 | tf_op jit(solution)/shard_map/all_to_all | solution.py:12
  92.6 400.6 %all-to-all-start.2 = ((f32[16,2,640,320]{2,3,1,0:T(8,128)}), f32[16,2,640,320]{2,3,1,0:T(8,128)}, u32[]{:S(2)}, u32[]{:S(2)}) async-start(f32[16,2,640,320]{2,3,1,0:T(8,128)} %stack.5), calls=%async_computation.2 | async-start | bytes 52428800 | tf_op jit(solution)/shard_map/all_to_all | solution.py:7
  99.4 490.3 %reduce-scatter.2.cloned.1.call-start = ((), (), s32[]{:S(2)}) async-start(), calls=%async_computation.4 | async-start | bytes 11796480 | tf_op jit(solution)/shard_map/reduce_scatter | solution.py:21
  531.2 58.5 %copy-start.1 = (f32[2,5120]{1,0:T(2,128)S(1)}, f32[2,5120]{1,0:T(2,128)}, u32[]{:S(2)}) copy-start(f32[2,5120]{1,0:T(2,128)} %param.7) | copy-start | bytes 122884
  531.2 58.5 %copy-start.2 = (f32[2,32]{1,0:T(2,128)S(1)}, f32[2,32]{1,0:T(2,128)}, u32[]{:S(2)}) copy-start(f32[2,32]{1,0:T(2,128)} %param.6) | copy-start | bytes 772
Sparse Core Ops, SparseCore 0:
  531.4 58.3 reduce-scatter.1
